TPU v7x, 512 devices: a whole 4x4x16 slice. The times are simulated.
512 devices in a mesh: blk: 64 (over z, x_lo, core), red: 8 (over x_hi, y).
Axes of the slice: x: 4 (x_hi: 2, x_lo: 2; x = x_hi * 2 + x_lo), y: 4, z: 16, core: 2. Of those that a mesh axis runs over, the one named last changes fastest.
Arguments:
- amplitudes: float32 [16384, 6144], P('blk', 'red'), may hold values from -6 to 6
- integrals: float32 [16384, 6144], P('blk', 'red'), may hold values from -0.21875 to 0.21875
- cd_irrep: int32 [8, 768], P('red'), may hold values from 0 to 7, never falling along the last dimension, each value on 1 to 192 neighbouring positions
- ab_irrep: int32 [64, 256], P('blk'), may hold values from 0 to 7, never falling along the last dimension, each value on 1 to 64 neighbouring positions
- ij_irrep: int32 [64, 256], P('blk'), may hold values from 0 to 7, never falling along the last dimension, each value on 1 to 64 neighbouring positions
Outputs:
- ladder: float32 [4, 16384, 256], P(None, ('blk', 'red'))
Inputs may be any that keep to these rules, and one draw needn't show every extreme that they name: `cd_irrep`: each row's labels never fall, every irrep 0 to 7 occurs in every row, and each irrep holds at most 192 positions of a row, exactly that many for some irrep. `ab_irrep`: each row's labels never fall, every irrep 0 to 7 occurs in every row, and each irrep holds at most 64 positions of a row, exactly that many for some irrep. `ij_irrep`: each row's labels never fall, every irrep 0 to 7 occurs in every row, and each irrep holds at most 64 positions of a row, exactly that many for some irrep.
All inputs are finite; a program needn't handle non-finite values.
Results may differ from a plain program's by a relative error of at most 0.0003.
Values sent between devices are 32-bit elements; how exact they have to be, the bound alone decides.
A program may use at most 64 MiB of HBM per device.

v0:
```python
import jax
import jax.numpy as jnp
from jax import lax
from jax.sharding import PartitionSpec as P

SHIFTS = 4


def cut_along(shard, dim, count):
    lengths = shard.shape
    blocks = shard.reshape(*lengths[:dim], count, lengths[dim] // count, *lengths[dim + 1 :])
    return jnp.moveaxis(blocks, dim, 0)


def summed_on_arrival(shard, axis, dim):
    blocks = cut_along(shard, dim, lax.axis_size(axis))
    arrived = lax.all_to_all(blocks, axis, split_axis=0, concat_axis=0, tiled=True)
    return arrived.sum(axis=0)


def shifted(shard, axis, by):
    count = lax.axis_size(axis)
    return lax.ppermute(shard, axis, [(i, (i + by) % count) for i in range(count)])


def screen_slab(amp_slab, slab_labels, cd_labels):
    return jnp.where(slab_labels[0][:, None] == cd_labels[0][None, :], amp_slab, jnp.float32(0.0))


def make_term(row_block, block_labels, screened, slab_labels):

    def term(start, count):
        row_labels = block_labels[0]
        product = lax.dot_general(
            row_block,
            screened,
            (((1,), (1,)), ((), ())),
            precision=lax.Precision.HIGHEST,
            preferred_element_type=jnp.float32,
        )
        return jnp.where(row_labels[:, None] == slab_labels[0][None, :], product, jnp.float32(0.0))

    return term


def reduce_terms(term_list, row_count):
    local_rows = row_count // lax.axis_size("red")
    start = jnp.int32(0)
    stacked = summed_on_arrival(
        jnp.stack([term(start, local_rows * lax.axis_size("red")) for term in term_list], axis=1),
        "red",
        0,
    )
    summed = [stacked[:, index] for index in range(len(term_list))]
    return summed


def body(amplitudes, integrals, cd_irrep, ab_irrep, ij_irrep):
    term_list = []
    slab_now, labels_now = (amplitudes, ij_irrep)
    for shift in range(SHIFTS):
        if shift > 0:
            slab_now, labels_now = shifted((slab_now, labels_now), "blk", 1)
        screened = screen_slab(slab_now, labels_now, cd_irrep)
        term_list.append(make_term(integrals, ab_irrep, screened, labels_now))
    results = reduce_terms(term_list, integrals.shape[0])
    return jnp.stack(results, 0)


def solution(mesh):
    in_specs = (P("blk", "red"), P("blk", "red"), P("red", None), P("blk", None), P("blk", None))
    out_specs = P(None, ("blk", "red"), None)
    return jax.shard_map(body, mesh=mesh, in_specs=in_specs, out_specs=out_specs, check_vma=False)
```

profile of v0, /device:TPU:8, one launch (start us, length us, event | category | flops | bytes accessed | tf_op | source)
XLA Modules:
  0.0 74.5 jit_solution(2247314741004931887)
XLA Ops:
  0.0 0.0 copy-start
  0.0 2.0 %collective-permute-start.1 = (f32[256,768]{1,0:T(8,128)}, f32[256,768]{1,0:T(8,128)S(1)}, u32[]{:S(2)}, u32[]{:S(2)}) collective-permute-start(f32[256,768]{1,0:T(8,128)} %param.5), channel_id=1, source_target_pairs={{0,8},{8,16},{16,24},{24,32},{32,40},{40,48},{48,56},{56,64},{64,7... | collective-permute-start | bytes 2359304 | tf_op jit(solution)/shard_map/ppermute | solution.py:23
  2.1 19.7 %collective-permute-done.1 = f32[256,768]{1,0:T(8,128)S(1)} collective-permute-done((f32[256,768]{1,0:T(8,128)}, f32[256,768]{1,0:T(8,128)S(1)}, u32[]{:S(2)}, u32[]{:S(2)}) %collective-permute-start.1) | collective-permute-done | bytes 786464 | tf_op jit(solution)/shard_map/ppermute | solution.py:23
  21.8 1.9 %collective-permute-start.3 = (f32[256,768]{1,0:T(8,128)S(1)}, f32[256,768]{1,0:T(8,128)S(1)}, u32[]{:S(2)}, u32[]{:S(2)}) collective-permute-start(f32[256,768]{1,0:T(8,128)S(1)} %collective-permute-done.1), channel_id=1, source_target_pairs={{0,8},{8,16},{16,24},{24,32},{32,40},{40,48},{48,56},{56,64},{64,7... | collective-permute-start | bytes 2359304 | tf_op jit(solution)/shard_map/ppermute | solution.py:23
  23.7 1.9 %collective-permute-start = (s32[1,256]{1,0:T(1,128)}, s32[1,256]{1,0:T(1,128)S(1)}, u32[]{:S(2)}, u32[]{:S(2)}) collective-permute-start(s32[1,256]{1,0:T(1,128)} %param.9), channel_id=1, source_target_pairs={{0,8},{8,16},{16,24},{24,32},{32,40},{40,48},{48,56},{56,64},{64,7... | collective-permute-start | bytes 3080 | tf_op jit(solution)/shard_map/ppermute | solution.py:23
  25.6 0.7 reduce
  26.3 10.9 %collective-permute-done = s32[1,256]{1,0:T(1,128)S(1)} collective-permute-done((s32[1,256]{1,0:T(1,128)}, s32[1,256]{1,0:T(1,128)S(1)}, u32[]{:S(2)}, u32[]{:S(2)}) %collective-permute-start) | collective-permute-done | bytes 1056 | tf_op jit(solution)/shard_map/ppermute | solution.py:23
  37.2 1.9 %collective-permute-start.2 = (s32[1,256]{1,0:T(1,128)S(1)}, s32[1,256]{1,0:T(1,128)S(1)}, u32[]{:S(2)}, u32[]{:S(2)}) collective-permute-start(s32[1,256]{1,0:T(1,128)S(1)} %collective-permute-done), channel_id=1, source_target_pairs={{0,8},{8,16},{16,24},{24,32},{32,40},{40,48},{48,56},{56,64},{64,7... | collective-permute-start | bytes 3080 | tf_op jit(solution)/shard_map/ppermute | solution.py:23
  39.1 0.0 collective-permute-done.3
  39.2 1.9 %collective-permute-start.5 = (f32[256,768]{1,0:T(8,128)S(1)}, f32[256,768]{1,0:T(8,128)S(1)}, u32[]{:S(2)}, u32[]{:S(2)}) collective-permute-start(f32[256,768]{1,0:T(8,128)S(1)} %collective-permute-done.3), channel_id=1, source_target_pairs={{0,8},{8,16},{16,24},{24,32},{32,40},{40,48},{48,56},{56,64},{64,7... | collective-permute-start | bytes 2359304 | tf_op jit(solution)/shard_map/ppermute | solution.py:23
  41.1 0.0 copy-start.2
  41.1 0.0 copy-start.1
  41.1 0.0 copy-done
  41.1 0.6 copy-done.2
  41.8 0.0 copy-done.1
  41.8 2.1 %fusion = f32[256,256]{1,0:T(8,128)S(1)} fusion(f32[256,768]{1,0:T(8,128)S(1)} %copy-done, f32[256,768]{1,0:T(8,128)} %param.5, s32[768]{0:T(1024)S(1)} %reduce, s32[256]{0:T(256)S(1)} %bitcast.53, s32[256]{0:T(256)S(1)} %bitcast.49), kind=kOutput, calls=%fused_computation.4 | convolution fusion | flops 604504064 | bytes 1840128 | tf_op jit(solution)/shard_map/dot_general | solution.py:34
  43.9 0.3 collective-permute-done.2
  44.2 1.9 %collective-permute-start.4 = (s32[1,256]{1,0:T(1,128)S(1)}, s32[1,256]{1,0:T(1,128)S(1)}, u32[]{:S(2)}, u32[]{:S(2)}) collective-permute-start(s32[1,256]{1,0:T(1,128)S(1)} %collective-permute-done.2), channel_id=1, source_target_pairs={{0,8},{8,16},{16,24},{24,32},{32,40},{40,48},{48,56},{56,64},{64,7... | collective-permute-start | bytes 3080 | tf_op jit(solution)/shard_map/ppermute | solution.py:23
  46.1 1.0 %compare_select_fusion.2 = f32[256,256]{1,0:T(8,128)S(1)} fusion(s32[256]{0:T(256)S(1)} %bitcast.54, s32[256]{0:T(256)S(1)} %bitcast.50, f32[256,768]{1,0:T(8,128)S(1)} %copy-done, f32[256,768]{1,0:T(8,128)S(1)} %collective-permute-done.1, s32[768]{0:T(1024)S(1)} %reduce), kind=kOutput, calls=%fused_computation.28 | convolution fusion | flops 604504064 | bytes 1840128 | tf_op jit(solution)/shard_map/dot_general | solution.py:34
  47.1 1.0 %compare_select_fusion.1 = f32[256,256]{1,0:T(8,128)S(1)} fusion(s32[256]{0:T(256)S(1)} %bitcast.55, s32[256]{0:T(256)S(1)} %bitcast.51, f32[256,768]{1,0:T(8,128)S(1)} %copy-done, f32[256,768]{1,0:T(8,128)S(1)} %collective-permute-done.3, s32[768]{0:T(1024)S(1)} %reduce), kind=kOutput, calls=%fused_computation.27 | convolution fusion | flops 604504064 | bytes 1840128 | tf_op jit(solution)/shard_map/dot_general | solution.py:34
  48.1 6.7 %collective-permute-done.4 = s32[1,256]{1,0:T(1,128)S(1)} collective-permute-done((s32[1,256]{1,0:T(1,128)S(1)}, s32[1,256]{1,0:T(1,128)S(1)}, u32[]{:S(2)}, u32[]{:S(2)}) %collective-permute-start.4) | collective-permute-done | bytes 1056 | tf_op jit(solution)/shard_map/ppermute | solution.py:23
  54.7 0.0 collective-permute-done.5
  54.7 0.9 %compare_select_fusion = f32[256,256]{1,0:T(8,128)S(1)} fusion(s32[256]{0:T(256)S(1)} %bitcast.56, s32[256]{0:T(256)S(1)} %bitcast.52, f32[256,768]{1,0:T(8,128)S(1)} %copy-done, f32[256,768]{1,0:T(8,128)S(1)} %collective-permute-done.5, s32[768]{0:T(1024)S(1)} %reduce), kind=kOutput, calls=%fused_computation.26 | convolution fusion | flops 604504064 | bytes 1840128 | tf_op jit(solution)/shard_map/dot_general | solution.py:34
  55.7 0.1 pad_maximum_fusion
  55.8 18.0 %all_to_all.5 = f32[8,32,4,256]{3,1,2,0:T(8,128)S(1)} all-to-all(f32[8,32,4,256]{3,1,2,0:T(8,128)S(1)} %pad_maximum_fusion), channel_id=1, replica_groups=mesh['blk'=64,'red'=8] {'red'}, dimensions={0} | all-to-all | bytes 2097152 | tf_op jit(solution)/shard_map/all_to_all | solution.py:17
  73.8 0.1 reduce_sum.9
  73.9 0.7 pad_maximum_fusion.1
  (1 shorter events, 0.0 us)
Async XLA Ops:
  0.0 41.1 %copy-start = (f32[256,768]{1,0:T(8,128)S(1)}, f32[256,768]{1,0:T(8,128)}, u32[]{:S(2)}) copy-start(f32[256,768]{1,0:T(8,128)} %param.6) | copy-start | bytes 2359300
  0.0 21.8 %collective-permute-start.1 = (f32[256,768]{1,0:T(8,128)}, f32[256,768]{1,0:T(8,128)S(1)}, u32[]{:S(2)}, u32[]{:S(2)}) collective-permute-start(f32[256,768]{1,0:T(8,128)} %param.5), channel_id=1, source_target_pairs={{0,8},{8,16},{16,24},{24,32},{32,40},{40,48},{48,56},{56,64},{64,7... | collective-permute-start | bytes 2359304 | tf_op jit(solution)/shard_map/ppermute | solution.py:23
  21.8 17.4 %collective-permute-start.3 = (f32[256,768]{1,0:T(8,128)S(1)}, f32[256,768]{1,0:T(8,128)S(1)}, u32[]{:S(2)}, u32[]{:S(2)}) collective-permute-start(f32[256,768]{1,0:T(8,128)S(1)} %collective-permute-done.1), channel_id=1, source_target_pairs={{0,8},{8,16},{16,24},{24,32},{32,40},{40,48},{48,56},{56,64},{64,7... | collective-permute-start | bytes 2359304 | tf_op jit(solution)/shard_map/ppermute | solution.py:23
  23.7 13.5 %collective-permute-start = (s32[1,256]{1,0:T(1,128)}, s32[1,256]{1,0:T(1,128)S(1)}, u32[]{:S(2)}, u32[]{:S(2)}) collective-permute-start(s32[1,256]{1,0:T(1,128)} %param.9), channel_id=1, source_target_pairs={{0,8},{8,16},{16,24},{24,32},{32,40},{40,48},{48,56},{56,64},{64,7... | collective-permute-start | bytes 3080 | tf_op jit(solution)/shard_map/ppermute | solution.py:23
  37.2 7.0 %collective-permute-start.2 = (s32[1,256]{1,0:T(1,128)S(1)}, s32[1,256]{1,0:T(1,128)S(1)}, u32[]{:S(2)}, u32[]{:S(2)}) collective-permute-start(s32[1,256]{1,0:T(1,128)S(1)} %collective-permute-done), channel_id=1, source_target_pairs={{0,8},{8,16},{16,24},{24,32},{32,40},{40,48},{48,56},{56,64},{64,7... | collective-permute-start | bytes 3080 | tf_op jit(solution)/shard_map/ppermute | solution.py:23
  39.2 15.6 %collective-permute-start.5 = (f32[256,768]{1,0:T(8,128)S(1)}, f32[256,768]{1,0:T(8,128)S(1)}, u32[]{:S(2)}, u32[]{:S(2)}) collective-permute-start(f32[256,768]{1,0:T(8,128)S(1)} %collective-permute-done.3), channel_id=1, source_target_pairs={{0,8},{8,16},{16,24},{24,32},{32,40},{40,48},{48,56},{56,64},{64,7... | collective-permute-start | bytes 2359304 | tf_op jit(solution)/shard_map/ppermute | solution.py:23
  41.1 0.7 copy-start.2
  41.1 0.7 copy-start.1
  44.2 10.5 %collective-permute-start.4 = (s32[1,256]{1,0:T(1,128)S(1)}, s32[1,256]{1,0:T(1,128)S(1)}, u32[]{:S(2)}, u32[]{:S(2)}) collective-permute-start(s32[1,256]{1,0:T(1,128)S(1)} %collective-permute-done.2), channel_id=1, source_target_pairs={{0,8},{8,16},{16,24},{24,32},{32,40},{40,48},{48,56},{56,64},{64,7... | collective-permute-start | bytes 3080 | tf_op jit(solution)/shard_map/ppermute | solution.py:23
where the time goes:
time: 74.9 us; the launch traced here: 74.5 us
  waiting for transfers between devices  37.7 us (50%)
  blocking collectives  18 us (24%)
  starting transfers between devices  11.6 us (15%)
  matrix products  4.93 us (7%)
  other arithmetic  1.54 us (2%)
    ppermute x6, waiting for transfers between devices, shifted(): lax.ppermute(shard, axis, [(i, (i + by) % count) for i in range(count)])  37.7 us
    all_to_all x1, blocking collectives, summed_on_arrival(): lax.all_to_all(blocks, axis, split_axis=0, concat_axis=0, tiled=True)  18 us
    ppermute x6, starting transfers between devices, shifted(): lax.ppermute(shard, axis, [(i, (i + by) % count) for i in range(count)])  11.6 us
    dot_general x4, matrix products, term(): lax.dot_general(row_block, screened, (((1,), (1,)), ((), ())), precision=...  4.93 us
  transfers between devices with their start and end apart: 6, of which 4 were waited for; matrix products, arithmetic and copies ran while one was open for 6% of the time, Pallas kernels for 0%

commit v1 on v0

v1 whole, which is shorter than its diff:
```python
import functools

import jax
import jax.numpy as jnp
from jax import lax
from jax.experimental import pallas as pl
from jax.experimental.pallas import tpu as pltpu
from jax.sharding import PartitionSpec as P

SHIFTS = 4
MESH = pl.DeviceIdType.MESH
F32 = jnp.float32
BF16 = jnp.bfloat16
LANES = 128
HALF = 200


def lanes_below(rows):
    return lax.broadcasted_iota(jnp.int32, (rows, LANES), 1) < 64


def column_of(labels):
    return jnp.transpose(jnp.broadcast_to(labels.astype(F32), (LANES, LANES)))


def folded(ref, row, rows, own, cd_labels):
    def kept(t):
        value = ref[pl.ds(row, rows), t * LANES : (t + 1) * LANES]
        return jnp.where(own == cd_labels[:, t * LANES : (t + 1) * LANES], value, 0.0)

    f0, f1, f2 = (kept(t) + kept(t + 3) for t in range(3))
    low = lanes_below(rows)
    head = f0 + pltpu.roll(jnp.where(low, f2, f1), 64, 1)
    tail = jnp.where(low, f1, f2)
    return head, tail + pltpu.roll(tail, 64, 1)


def split(value):
    high = value.astype(BF16)
    return high, (value - high.astype(F32)).astype(BF16)


def kernel(
    n_blk, amp_hbm, int_hbm, cd_ref, ab_ref, ij_ref, out_ref,
    amp, integ, slabs, v_parts, ab_col, send, arrived, x_send, x_arrived,
    load_sem, own_send, own_recv, half_send, half_recv, fwd_send, fwd_recv,
    y_send, y_recv, xs_send, xs_recv,
):
    b, r = lax.axis_index("blk"), lax.axis_index("red")
    c = lax.rem(b, 2)
    y, x_hi = lax.rem(r, 4), r // 4
    partner = y + 4 * (1 - x_hi)

    def block(offset):
        return (lax.rem(b + offset + n_blk, n_blk), r)

    def red(k):
        return x_hi * 4 + lax.rem(y + k, 4)

    loads = [
        pltpu.make_async_copy(amp_hbm.at[pl.ds(128 * h, 128)], amp.at[pl.ds(128 * h, 128)], load_sem.at[h])
        for h in range(2)
    ] + [pltpu.make_async_copy(int_hbm, integ, load_sem.at[2])]
    for load in loads:
        load.start()

    barrier = pltpu.get_barrier_semaphore()
    for offset in (-3, -2, -1, 1):
        pl.semaphore_signal(barrier, inc=1, device_id=block(offset), device_id_type=MESH)
    for k in (1, 2, 3):
        pl.semaphore_signal(barrier, inc=1, device_id=(b, red(k)), device_id_type=MESH)
    pl.semaphore_signal(barrier, inc=1, device_id=(b, partner), device_id_type=MESH)

    cd_labels = cd_ref[...].astype(F32)
    for h in range(2):
        pair_labels = ij_ref[:, 128 * h : 128 * h + 128].astype(F32)
        own = column_of(pair_labels)
        loads[h].wait()
        tails = []
        for part in range(2):
            head, tail = folded(amp, 128 * h + 64 * part, 64, own[64 * part : 64 * part + 64], cd_labels)
            slabs[0, h, 64 * part : 64 * part + 64] = head
            tails.append(tail)
        slabs[0, h, 128:192] = jnp.where(lanes_below(64), *tails)
        slabs[0, h, 192:200] = jnp.broadcast_to(pair_labels, (8, LANES))

    pl.semaphore_wait(barrier, 8)

    def half_copy(h):
        return pltpu.make_async_remote_copy(
            src_ref=slabs.at[0, h], dst_ref=slabs.at[2 + h - c, h],
            send_sem=half_send.at[h], recv_sem=half_recv.at[1 - c],
            device_id=block(2 + h - c), device_id_type=MESH,
        )

    own_copy = pltpu.make_async_remote_copy(
        src_ref=slabs.at[0], dst_ref=slabs.at[1 + 2 * c],
        send_sem=own_send, recv_sem=own_recv,
        device_id=block(1 + 2 * c), device_id_type=MESH,
    )
    half_copy(0).start()
    half_copy(1).start()
    own_copy.start()

    def forward(i):
        return pltpu.make_async_remote_copy(
            src_ref=slabs.at[1 + i + c, c], dst_ref=slabs.at[2 + i - c, c],
            send_sem=fwd_send.at[i], recv_sem=fwd_recv.at[i],
            device_id=block(1 - 2 * c), device_id_type=MESH,
        )

    def half_arrival(i):
        return pltpu.make_async_remote_copy(
            src_ref=slabs.at[0, c], dst_ref=slabs.at[1 + i + c, c],
            send_sem=half_send.at[0], recv_sem=half_recv.at[i],
            device_id=block(2), device_id_type=MESH,
        )

    loads[2].wait()
    for h in range(2):
        own = column_of(ab_ref[:, 128 * h : 128 * h + 128])
        ab_col[128 * h : 128 * h + 128] = own
        for part in range(2):
            row = 128 * h + 64 * part
            head, tail = folded(integ, row, 64, own[64 * part : 64 * part + 64], cd_labels)
            for t, piece in enumerate((head, jnp.where(lanes_below(64), tail, 0.0))):
                high, low = split(piece)
                v_parts[row : row + 64, t * LANES : (t + 1) * LANES] = high
                v_parts[256 + row : 320 + row, t * LANES : (t + 1) * LANES] = low

    def dot(lhs, rhs):
        return lax.dot_general(lhs, rhs, (((1,), (1,)), ((), ())), preferred_element_type=F32)

    def y_copy(m, k):
        return pltpu.make_async_remote_copy(
            src_ref=send.at[m, lax.rem(y + k, 4)], dst_ref=arrived.at[m, k - 1],
            send_sem=y_send.at[m, k - 1], recv_sem=y_recv.at[m, k - 1],
            device_id=(b, red(k)), device_id_type=MESH,
        )

    def process(m):
        low = lanes_below(64)
        parts = []
        for h in range(2):
            tail = slabs[m, h, 128:192]
            parts.append(jnp.concatenate([slabs[m, h, 0:64], tail], axis=1))
            parts.append(jnp.concatenate([slabs[m, h, 64:128], pltpu.roll(tail, 64, 1)], axis=1))
        high, rest = split(jnp.concatenate(parts, axis=0))
        both = dot(v_parts[...], high)
        product = both[:256] + both[256:] + dot(v_parts[:256], rest)
        masked = jnp.zeros((256, LANES), F32)
        for h in range(2):
            mask = ab_col[...] == slabs[m, h, 192:193]
            masked = masked + jnp.where(mask, product[:, 128 * h : 128 * h + 128], 0.0)
        twice = masked + pltpu.roll(masked, 64, 1)
        low = lanes_below(16)
        for block_row in range(8):
            row = 32 * block_row
            packed = jnp.where(low, twice[row : row + 16], twice[row + 16 : row + 32])
            send[m, block_row % 4, 16 * (block_row // 4) : 16 * (block_row // 4) + 16] = packed
        for k in (1, 2, 3):
            y_copy(m, k).start()

    def x_copy(m):
        return pltpu.make_async_remote_copy(
            src_ref=x_send.at[m, 1 - x_hi], dst_ref=x_arrived.at[m],
            send_sem=xs_send.at[m], recv_sem=xs_recv.at[m],
            device_id=(b, partner), device_id_type=MESH,
        )

    def along_y(m):
        total = send[m, y]
        for k in (1, 2, 3):
            y_copy(m, k).wait_recv()
            total = total + arrived[m, k - 1]
        x_send[m, 0] = total[:16]
        x_send[m, 1] = total[16:]
        x_copy(m).start()

    def finish(m):
        x_copy(m).wait_recv()
        total = x_send[m, x_hi] + x_arrived[m]
        turned = pltpu.roll(total, 64, 1)
        low = lanes_below(16)
        first, second = jnp.where(low, total, turned), jnp.where(low, turned, total)
        rows = jnp.concatenate([first, second], axis=0)
        own = ab_col[pl.ds(pl.multiple_of(32 * r, 32), 32)]
        for h in range(2):
            mask = own == slabs[m, h, 192:193]
            out_ref[m, :, 128 * h : 128 * h + 128] = jnp.where(mask, rows, 0.0)

    first, second, third = 3 - 2 * c, 1 + c, 2 + c
    process(0)
    half_arrival(0).wait_recv()
    forward(0).start()
    half_arrival(1).wait_recv()
    forward(1).start()
    own_copy.wait_recv()
    process(first)
    along_y(0)
    forward(0).wait_recv()
    process(second)
    along_y(first)
    forward(1).wait_recv()
    process(third)
    finish(0)
    along_y(second)
    finish(first)
    along_y(third)
    finish(second)
    finish(third)

    own_copy.wait_send()
    for i in range(2):
        half_copy(i).wait_send()
        forward(i).wait_send()
    for m in range(SHIFTS):
        for k in (1, 2, 3):
            y_copy(m, k).wait_send()
        x_copy(m).wait_send()


def solution(mesh):
    n_blk = mesh.shape["blk"]

    def body(amplitudes, integrals, cd_irrep, ab_irrep, ij_irrep):
        vmem = pl.BlockSpec(memory_space=pltpu.VMEM)
        hbm = pl.BlockSpec(memory_space=pl.ANY)
        return pl.pallas_call(
            functools.partial(kernel, n_blk),
            out_shape=jax.ShapeDtypeStruct((SHIFTS, 32, 256), F32),
            in_specs=[hbm, hbm, vmem, vmem, vmem],
            out_specs=vmem,
            scratch_shapes=[
                pltpu.VMEM((256, 768), F32),
                pltpu.VMEM((256, 768), F32),
                pltpu.VMEM((SHIFTS, 2, HALF, LANES), F32),
                pltpu.VMEM((512, 256), BF16),
                pltpu.VMEM((256, LANES), F32),
                pltpu.VMEM((SHIFTS, 4, 32, LANES), F32),
                pltpu.VMEM((SHIFTS, 3, 32, LANES), F32),
                pltpu.VMEM((SHIFTS, 2, 16, LANES), F32),
                pltpu.VMEM((SHIFTS, 16, LANES), F32),
                pltpu.SemaphoreType.DMA((3,)),
                pltpu.SemaphoreType.DMA,
                pltpu.SemaphoreType.DMA,
                pltpu.SemaphoreType.DMA((2,)),
                pltpu.SemaphoreType.DMA((2,)),
                pltpu.SemaphoreType.DMA((2,)),
                pltpu.SemaphoreType.DMA((2,)),
                pltpu.SemaphoreType.DMA((SHIFTS, 3)),
                pltpu.SemaphoreType.DMA((SHIFTS, 3)),
                pltpu.SemaphoreType.DMA((SHIFTS,)),
                pltpu.SemaphoreType.DMA((SHIFTS,)),
            ],
            compiler_params=pltpu.CompilerParams(collective_id=0, has_side_effects=True),
        )(amplitudes, integrals, cd_irrep, ab_irrep, ij_irrep)

    in_specs = (P("blk", "red"), P("blk", "red"), P("red", None), P("blk", None), P("blk", None))
    out_specs = P(None, ("blk", "red"), None)
    return jax.shard_map(body, mesh=mesh, in_specs=in_specs, out_specs=out_specs, check_vma=False)
```

time: 74.9 us -> 36.1 us (0.48)
  the two profiles are of different devices: /device:TPU:8 before, /device:TPU:2 now
where the time goes in v1:
time: 36.1 us; the launch traced here: 35.9 us
  Pallas kernels  34.3 us (95%)
  local copies, waits for them, and re-layouts  1.57 us (4%)
    pallas_call x1, Pallas kernels, body(): pl.pallas_call(functools.partial(kernel, n_blk), out_shape=jax.ShapeDtype...  34.3 us
    unnamed x1, local copies, waits for them, and re-layouts  1.57 us

profile of v1, /device:TPU:2, one launch (start us, length us, event | category | flops | bytes accessed | tf_op | source)
XLA Modules:
  0.0 35.9 jit_solution(8924985647914179402)
XLA Ops:
  0.0 34.3 %shard_map.55 = f32[4,32,256]{2,1,0:T(8,128)} custom-call(f32[256,768]{1,0:T(8,128)} %amp_hbm.1, f32[256,768]{1,0:T(8,128)} %int_hbm.1, s32[1,768]{1,0:T(1,128)} %cd_ref.1, s32[1,256]{1,0:T(1,128)} %ab_ref.1, s32[1,256]{1,0:T(1,128)} %ij_ref.1), custom_call_target="tpu_custom_call" | custom-call | tf_op jit(solution)/shard_map/pallas_call | solution.py:229
  34.3 1.6 %copy.7 = f32[4,32,256]{2,1,0:T(8,128)} copy(f32[4,32,256]{2,1,0:T(8,128)} %shard_map.55) | data formatting | bytes 262144

commit v2 on v1

v2 whole, which is shorter than its diff:
```python
import functools

import jax
import jax.numpy as jnp
from jax import lax
from jax.experimental import pallas as pl
from jax.experimental.pallas import tpu as pltpu
from jax.sharding import PartitionSpec as P

SHIFTS = 4
MESH = pl.DeviceIdType.MESH
F32 = jnp.float32
BF16 = jnp.bfloat16
LANES = 128
VMEM_LIMIT = 60 * 1024 * 1024
HALF = 200


def lanes_below(rows):
    return lax.broadcasted_iota(jnp.int32, (rows, LANES), 1) < 64


def column_of(labels):
    return jnp.transpose(jnp.broadcast_to(labels.astype(F32), (LANES, LANES)))


def folded(ref, row, rows, own, cd_labels):
    def kept(t):
        value = ref[pl.ds(row, rows), t * LANES : (t + 1) * LANES]
        return jnp.where(own == cd_labels[:, t * LANES : (t + 1) * LANES], value, 0.0)

    f0, f1, f2 = (kept(t) + kept(t + 3) for t in range(3))
    low = lanes_below(rows)
    head = f0 + pltpu.roll(jnp.where(low, f2, f1), 64, 1)
    tail = jnp.where(low, f1, f2)
    return head, tail + pltpu.roll(tail, 64, 1)


def split(value):
    high = value.astype(BF16)
    return high, (value - high.astype(F32)).astype(BF16)


def kernel(
    n_blk, amp_hbm, int_hbm, cd_hbm, ab_hbm, ij_hbm, out_ref,
    amp, integ, cd, ab, ij, slabs, v_parts, ab_col, send, arrived,
    load_sem, ready_sem, own_send, own_recv, half_send, half_recv, fwd_send, fwd_recv, red_send, red_recv,
):
    loads = [
        pltpu.make_async_copy(src, dst, load_sem.at[i])
        for i, (src, dst) in enumerate((
            (ij_hbm, ij),
            (cd_hbm, cd),
            (amp_hbm.at[pl.ds(0, 128)], amp.at[pl.ds(0, 128)]),
            (amp_hbm.at[pl.ds(128, 128)], amp.at[pl.ds(128, 128)]),
            (ab_hbm, ab),
            (int_hbm, integ),
        ))
    ]
    for load in loads:
        load.start()

    b, r = lax.axis_index("blk"), lax.axis_index("red")
    c = lax.rem(b, 2)
    y, x_hi = lax.rem(r, 4), r // 4

    def block(offset):
        return (lax.rem(b + offset + n_blk, n_blk), r)

    def red(x_step, y_step):
        x_to = 1 - x_hi if x_step else x_hi
        return (b, x_to * 4 + lax.rem(y + y_step, 4))

    barrier = pltpu.get_barrier_semaphore()
    for offset in (-3, -2, -1, 1):
        pl.semaphore_signal(barrier, inc=1, device_id=block(offset), device_id_type=MESH)
    for steps in ((0, 1), (0, 2), (0, 3), (1, 0)):
        pl.semaphore_signal(barrier, inc=1, device_id=red(*steps), device_id_type=MESH)

    loads[0].wait()
    loads[1].wait()
    cd_labels = cd[...].astype(F32)
    for h in range(2):
        pair_labels = ij[:, 128 * h : 128 * h + 128].astype(F32)
        own = column_of(pair_labels)
        loads[2 + h].wait()
        tails = []
        for part in range(2):
            head, tail = folded(amp, 128 * h + 64 * part, 64, own[64 * part : 64 * part + 64], cd_labels)
            slabs[0, h, 64 * part : 64 * part + 64] = head
            tails.append(tail)
        slabs[0, h, 128:192] = jnp.where(lanes_below(64), *tails)
        slabs[0, h, 192:200] = jnp.broadcast_to(pair_labels, (8, LANES))

    pl.semaphore_wait(barrier, 8)

    def half_copy(h):
        return pltpu.make_async_remote_copy(
            src_ref=slabs.at[0, h], dst_ref=slabs.at[2 + h - c, h],
            send_sem=half_send.at[h], recv_sem=half_recv.at[1 - c],
            device_id=block(2 + h - c), device_id_type=MESH,
        )

    own_copy = pltpu.make_async_remote_copy(
        src_ref=slabs.at[0], dst_ref=slabs.at[1 + 2 * c],
        send_sem=own_send, recv_sem=own_recv,
        device_id=block(1 + 2 * c), device_id_type=MESH,
    )
    half_copy(0).start()
    half_copy(1).start()
    own_copy.start()
    for y_step in (1, 2, 3):
        pl.semaphore_signal(ready_sem, inc=1, device_id=red(0, y_step), device_id_type=MESH)

    def forward(i):
        return pltpu.make_async_remote_copy(
            src_ref=slabs.at[1 + i + c, c], dst_ref=slabs.at[2 + i - c, c],
            send_sem=fwd_send.at[i], recv_sem=fwd_recv.at[i],
            device_id=block(1 - 2 * c), device_id_type=MESH,
        )

    def half_arrival(i):
        return pltpu.make_async_remote_copy(
            src_ref=slabs.at[0, c], dst_ref=slabs.at[1 + i + c, c],
            send_sem=half_send.at[0], recv_sem=half_recv.at[i],
            device_id=block(2), device_id_type=MESH,
        )

    loads[4].wait()
    loads[5].wait()
    for h in range(2):
        own = column_of(ab[:, 128 * h : 128 * h + 128])
        ab_col[128 * h : 128 * h + 128] = own
        for part in range(2):
            row = 128 * h + 64 * part
            head, tail = folded(integ, row, 64, own[64 * part : 64 * part + 64], cd_labels)
            for t, piece in enumerate((head, jnp.where(lanes_below(64), tail, 0.0))):
                high, low = split(piece)
                v_parts[row : row + 64, t * LANES : (t + 1) * LANES] = high
                v_parts[256 + row : 320 + row, t * LANES : (t + 1) * LANES] = low

    def dot(lhs, rhs):
        return lax.dot_general(lhs, rhs, (((1,), (1,)), ((), ())), preferred_element_type=F32)

    def to_peers(m):
        for x_step in range(2):
            for y_step in range(4):
                if x_step or y_step:
                    to = red(x_step, y_step)
                    pltpu.make_async_remote_copy(
                        src_ref=send.at[m, to[1]], dst_ref=arrived.at[m, 4 * x_step + y_step - 1],
                        send_sem=red_send.at[m], recv_sem=red_recv.at[m],
                        device_id=to, device_id_type=MESH,
                    ).start()

    def all_peers(m):
        return pltpu.make_async_remote_copy(
            src_ref=arrived.at[m], dst_ref=arrived.at[m],
            send_sem=red_send.at[m], recv_sem=red_recv.at[m],
            device_id=red(1, 0), device_id_type=MESH,
        )

    def process(m):
        parts = []
        for h in range(2):
            tail = slabs[m, h, 128:192]
            parts.append(jnp.concatenate([slabs[m, h, 0:64], tail], axis=1))
            parts.append(jnp.concatenate([slabs[m, h, 64:128], pltpu.roll(tail, 64, 1)], axis=1))
        high, rest = split(jnp.concatenate(parts, axis=0))
        both = dot(v_parts[...], high)
        product = both[:256] + both[256:] + dot(v_parts[:256], rest)
        masked = jnp.zeros((256, LANES), F32)
        for h in range(2):
            mask = ab_col[...] == slabs[m, h, 192:193]
            masked = masked + jnp.where(mask, product[:, 128 * h : 128 * h + 128], 0.0)
        twice = masked + pltpu.roll(masked, 64, 1)
        low = lanes_below(16)
        for block_row in range(8):
            row = 32 * block_row
            send[m, block_row] = jnp.where(low, twice[row : row + 16], twice[row + 16 : row + 32])

    def finish(m):
        all_peers(m).wait_recv()
        total = send[m, r]
        for i in range(7):
            total = total + arrived[m, i]
        turned = pltpu.roll(total, 64, 1)
        low = lanes_below(16)
        rows = jnp.concatenate([jnp.where(low, total, turned), jnp.where(low, turned, total)], axis=0)
        own = ab_col[pl.ds(pl.multiple_of(32 * r, 32), 32)]
        for h in range(2):
            mask = own == slabs[m, h, 192:193]
            out_ref[m, :, 128 * h : 128 * h + 128] = jnp.where(mask, rows, 0.0)

    first, second, third = 3 - 2 * c, 1 + c, 2 + c

    process(0)
    pl.semaphore_wait(ready_sem, 3)
    to_peers(0)

    @pl.when(c == 1)
    def _():
        own_copy.wait_recv()
        process(first)
        to_peers(first)

    half_arrival(0).wait_recv()
    forward(0).start()
    half_arrival(1).wait_recv()
    forward(1).start()
    forward(0).wait_recv()
    process(second)
    to_peers(second)
    forward(1).wait_recv()
    process(third)
    to_peers(third)

    @pl.when(c == 0)
    def _():
        own_copy.wait_recv()
        process(first)
        to_peers(first)

    finish(0)

    @pl.when(c == 1)
    def _():
        finish(first)

    finish(second)
    finish(third)

    @pl.when(c == 0)
    def _():
        finish(first)

    own_copy.wait_send()
    for i in range(2):
        half_copy(i).wait_send()
        forward(i).wait_send()
    for m in range(SHIFTS):
        all_peers(m).wait_send()


def solution(mesh):
    n_blk = mesh.shape["blk"]

    def body(amplitudes, integrals, cd_irrep, ab_irrep, ij_irrep):
        vmem = pl.BlockSpec(memory_space=pltpu.VMEM)
        hbm = pl.BlockSpec(memory_space=pltpu.HBM)
        return pl.pallas_call(
            functools.partial(kernel, n_blk),
            out_shape=jax.ShapeDtypeStruct((SHIFTS, 32, 256), F32),
            in_specs=[hbm] * 5,
            out_specs=vmem,
            scratch_shapes=[
                pltpu.VMEM((256, 768), F32),
                pltpu.VMEM((256, 768), F32),
                pltpu.VMEM((1, 768), jnp.int32),
                pltpu.VMEM((1, 256), jnp.int32),
                pltpu.VMEM((1, 256), jnp.int32),
                pltpu.VMEM((SHIFTS, 2, HALF, LANES), F32),
                pltpu.VMEM((512, 256), BF16),
                pltpu.VMEM((256, LANES), F32),
                pltpu.VMEM((SHIFTS, 8, 16, LANES), F32),
                pltpu.VMEM((SHIFTS, 7, 16, LANES), F32),
                pltpu.SemaphoreType.DMA((6,)),
                pltpu.SemaphoreType.REGULAR,
                pltpu.SemaphoreType.DMA,
                pltpu.SemaphoreType.DMA,
                pltpu.SemaphoreType.DMA((2,)),
                pltpu.SemaphoreType.DMA((2,)),
                pltpu.SemaphoreType.DMA((2,)),
                pltpu.SemaphoreType.DMA((2,)),
                pltpu.SemaphoreType.DMA((SHIFTS,)),
                pltpu.SemaphoreType.DMA((SHIFTS,)),
            ],
            compiler_params=pltpu.CompilerParams(
                collective_id=0, has_side_effects=True, vmem_limit_bytes=VMEM_LIMIT
            ),
        )(amplitudes, integrals, cd_irrep, ab_irrep, ij_irrep)

    in_specs = (P("blk", "red"), P("blk", "red"), P("red", None), P("blk", None), P("blk", None))
    out_specs = P(None, ("blk", "red"), None)
    return jax.shard_map(body, mesh=mesh, in_specs=in_specs, out_specs=out_specs, check_vma=False)
```

time: 36.1 us -> 29.4 us (0.81)
  the two profiles are of different devices: /device:TPU:2 before, /device:TPU:1 now
where the time goes in v2:
time: 29.4 us; the launch traced here: 29.2 us
  Pallas kernels  27.7 us (94%)
  local copies, waits for them, and re-layouts  1.57 us (5%)
    pallas_call x1, Pallas kernels, body(): pl.pallas_call(functools.partial(kernel, n_blk), out_shape=jax.ShapeDtype...  27.7 us
    unnamed x1, local copies, waits for them, and re-layouts  1.57 us

profile of v2, /device:TPU:1, one launch (start us, length us, event | category | flops | bytes accessed | tf_op | source)
XLA Modules:
  0.0 29.2 jit_solution(12557306682836796090)
XLA Ops:
  0.0 27.7 %shard_map.55 = f32[4,32,256]{2,1,0:T(8,128)} custom-call(f32[256,768]{1,0:T(8,128)} %amp_hbm.1, f32[256,768]{1,0:T(8,128)} %int_hbm.1, s32[1,768]{1,0:T(1,128)} %cd_hbm.1, s32[1,256]{1,0:T(1,128)} %ab_hbm.1, s32[1,256]{1,0:T(1,128)} %ij_hbm.1), custom_call_target="tpu_custom_call" | custom-call | tf_op jit(solution)/shard_map/pallas_call | solution.py:251
  27.7 1.6 %copy.7 = f32[4,32,256]{2,1,0:T(8,128)} copy(f32[4,32,256]{2,1,0:T(8,128)} %shard_map.55) | data formatting | bytes 262144

commit v3 on v2

--- a/solution.py
+++ b/solution.py
@@ -250,7 +250,7 @@
         hbm = pl.BlockSpec(memory_space=pltpu.HBM)
         return pl.pallas_call(
             functools.partial(kernel, n_blk),
-            out_shape=jax.ShapeDtypeStruct((SHIFTS, 32, 256), F32),
+            out_shape=pltpu.VMEM((SHIFTS, 32, 256), F32),
             in_specs=[hbm] * 5,
             out_specs=vmem,
             scratch_shapes=[

time: 29.4 us -> 27.8 us (0.946)
  local copies, waits for them, and re-layouts: 1.57 us -> 0.66 us
  Pallas kernels: 27.7 us -> 27 us
    unnamed x1, local copies, waits for them, and re-layouts: 1.57 us -> 0.66 us
    pallas_call x1, Pallas kernels: 27.7 us -> 27 us  [body(): pl.pallas_call(functools.partial(kernel, n_blk), out_shape=pltpu.VMEM((SH...]
where the time goes in v3:
time: 27.8 us; the launch traced here: 27.7 us
  Pallas kernels  27 us (97%)
  local copies, waits for them, and re-layouts  0.66 us (2%)
    pallas_call x1, Pallas kernels, body(): pl.pallas_call(functools.partial(kernel, n_blk), out_shape=pltpu.VMEM((SH...  27 us
    unnamed x1, local copies, waits for them, and re-layouts  0.66 us

profile of v3, /device:TPU:1, one launch (start us, length us, event | category | flops | bytes accessed | tf_op | source)
XLA Modules:
  0.0 27.7 jit_solution(507387010497391556)
XLA Ops:
  0.0 27.0 %shard_map.55 = f32[4,32,256]{2,1,0:T(8,128)S(1)} custom-call(f32[256,768]{1,0:T(8,128)} %amp_hbm.1, f32[256,768]{1,0:T(8,128)} %int_hbm.1, s32[1,768]{1,0:T(1,128)} %cd_hbm.1, s32[1,256]{1,0:T(1,128)} %ab_hbm.1, s32[1,256]{1,0:T(1,128)} %ij_hbm.1), custom_call_target="tpu_custom_call" | custom-call | tf_op jit(solution)/shard_map/pallas_call | solution.py:251
  27.0 0.7 %copy.7 = f32[4,32,256]{2,1,0:T(8,128)} copy(f32[4,32,256]{2,1,0:T(8,128)S(1)} %shard_map.55) | data formatting | bytes 262144

commit v4 on v3

--- a/solution.py
+++ b/solution.py
@@ -44,7 +44,8 @@
 def kernel(
     n_blk, amp_hbm, int_hbm, cd_hbm, ab_hbm, ij_hbm, out_ref,
     amp, integ, cd, ab, ij, slabs, v_parts, ab_col, send, arrived,
-    load_sem, ready_sem, own_send, own_recv, half_send, half_recv, fwd_send, fwd_recv, red_send, red_recv,
+    load_sem, ready_sem, own_send, own_recv, half_send, half_recv, fwd_send, fwd_recv,
+    pass_send, pass_recv, red_send, red_recv,
 ):
     loads = [
         pltpu.make_async_copy(src, dst, load_sem.at[i])
@@ -61,6 +62,7 @@
         load.start()
 
     b, r = lax.axis_index("blk"), lax.axis_index("red")
+    k = lax.rem(b, 4)
     c = lax.rem(b, 2)
     y, x_hi = lax.rem(r, 4), r // 4
 
@@ -78,19 +80,21 @@
         pl.semaphore_signal(barrier, inc=1, device_id=red(*steps), device_id_type=MESH)
 
     loads[0].wait()
+    pair_labels = [ij[:, 128 * h : 128 * h + 128].astype(F32) for h in range(2)]
+    pair_columns = [column_of(labels) for labels in pair_labels]
     loads[1].wait()
     cd_labels = cd[...].astype(F32)
+    loads[2].wait()
+    loads[3].wait()
     for h in range(2):
-        pair_labels = ij[:, 128 * h : 128 * h + 128].astype(F32)
-        own = column_of(pair_labels)
-        loads[2 + h].wait()
         tails = []
         for part in range(2):
-            head, tail = folded(amp, 128 * h + 64 * part, 64, own[64 * part : 64 * part + 64], cd_labels)
+            own = pair_columns[h][64 * part : 64 * part + 64]
+            head, tail = folded(amp, 128 * h + 64 * part, 64, own, cd_labels)
             slabs[0, h, 64 * part : 64 * part + 64] = head
             tails.append(tail)
         slabs[0, h, 128:192] = jnp.where(lanes_below(64), *tails)
-        slabs[0, h, 192:200] = jnp.broadcast_to(pair_labels, (8, LANES))
+        slabs[0, h, 192:200] = jnp.broadcast_to(pair_labels[h], (8, LANES))
 
     pl.semaphore_wait(barrier, 8)
 
@@ -106,9 +110,15 @@
         send_sem=own_send, recv_sem=own_recv,
         device_id=block(1 + 2 * c), device_id_type=MESH,
     )
-    half_copy(0).start()
-    half_copy(1).start()
-    own_copy.start()
+    @pl.when(k != 2)
+    def _():
+        half_copy(0).start()
+        half_copy(1).start()
+
+    @pl.when(k != 3)
+    def _():
+        own_copy.start()
+
     for y_step in (1, 2, 3):
         pl.semaphore_signal(ready_sem, inc=1, device_id=red(0, y_step), device_id_type=MESH)
 
@@ -117,6 +127,19 @@
             src_ref=slabs.at[1 + i + c, c], dst_ref=slabs.at[2 + i - c, c],
             send_sem=fwd_send.at[i], recv_sem=fwd_recv.at[i],
             device_id=block(1 - 2 * c), device_id_type=MESH,
+        )
+
+    pass_on = pltpu.make_async_remote_copy(
+        src_ref=slabs.at[1 + c, c], dst_ref=slabs.at[3, c],
+        send_sem=pass_send, recv_sem=pass_recv.at[c],
+        device_id=block(2 - c), device_id_type=MESH,
+    )
+
+    def passed(h):
+        return pltpu.make_async_remote_copy(
+            src_ref=slabs.at[0, h], dst_ref=slabs.at[3, h],
+            send_sem=pass_send, recv_sem=pass_recv.at[h],
+            device_id=block(-1), device_id_type=MESH,
         )
 
     def half_arrival(i):
@@ -143,8 +166,8 @@
         return lax.dot_general(lhs, rhs, (((1,), (1,)), ((), ())), preferred_element_type=F32)
 
     def to_peers(m):
-        for x_step in range(2):
-            for y_step in range(4):
+        for x_step in (1, 0):
+            for y_step in (2, 1, 3, 0):
                 if x_step or y_step:
                     to = red(x_step, y_step)
                     pltpu.make_async_remote_copy(
@@ -194,47 +217,83 @@
 
     first, second, third = 3 - 2 * c, 1 + c, 2 + c
 
+    def shift(m):
+        process(m)
+        to_peers(m)
+
+    def from_last_chip(i):
+        half_arrival(i).wait_recv()
+        forward(i).start()
+
     process(0)
     pl.semaphore_wait(ready_sem, 3)
     to_peers(0)
 
+    @pl.when(k == 2)
+    def _():
+        half_copy(0).start()
+        half_copy(1).start()
+
+    @pl.when(k == 0)
+    def _():
+        from_last_chip(0)
+        pass_on.start()
+        own_copy.wait_recv()
+        shift(3)
+        from_last_chip(1)
+        forward(0).wait_recv()
+        shift(1)
+        forward(1).wait_recv()
+        shift(2)
+        finish(0)
+        finish(3)
+        finish(1)
+        finish(2)
+
+    @pl.when(k == 2)
+    def _():
+        from_last_chip(0)
+        from_last_chip(1)
+        forward(0).wait_recv()
+        shift(1)
+        forward(1).wait_recv()
+        shift(2)
+        finish(0)
+        passed(0).wait_recv()
+        passed(1).wait_recv()
+        shift(3)
+        finish(1)
+        finish(2)
+        finish(3)
+
     @pl.when(c == 1)
     def _():
         own_copy.wait_recv()
-        process(first)
-        to_peers(first)
-
-    half_arrival(0).wait_recv()
-    forward(0).start()
-    half_arrival(1).wait_recv()
-    forward(1).start()
-    forward(0).wait_recv()
-    process(second)
-    to_peers(second)
-    forward(1).wait_recv()
-    process(third)
-    to_peers(third)
-
-    @pl.when(c == 0)
-    def _():
-        own_copy.wait_recv()
-        process(first)
-        to_peers(first)
-
-    finish(0)
-
-    @pl.when(c == 1)
-    def _():
-        finish(first)
-
-    finish(second)
-    finish(third)
-
-    @pl.when(c == 0)
-    def _():
-        finish(first)
-
-    own_copy.wait_send()
+        shift(1)
+        from_last_chip(0)
+
+        @pl.when(k == 1)
+        def _():
+            pass_on.start()
+
+        forward(0).wait_recv()
+        shift(2)
+        from_last_chip(1)
+        forward(1).wait_recv()
+        shift(3)
+        finish(0)
+        finish(1)
+        finish(2)
+        finish(3)
+
+    @pl.when(k != 3)
+    def _():
+        own_copy.wait_send()
+
+    @pl.when(k < 2)
+    def _():
+        pass_on.wait_send()
+
     for i in range(2):
         half_copy(i).wait_send()
         forward(i).wait_send()
@@ -272,6 +331,8 @@
                 pltpu.SemaphoreType.DMA((2,)),
                 pltpu.SemaphoreType.DMA((2,)),
                 pltpu.SemaphoreType.DMA((2,)),
+                pltpu.SemaphoreType.DMA,
+                pltpu.SemaphoreType.DMA((2,)),
                 pltpu.SemaphoreType.DMA((SHIFTS,)),
                 pltpu.SemaphoreType.DMA((SHIFTS,)),
             ],

time: 27.8 us -> 27.4 us (0.986)
  Pallas kernels: 27 us -> 26.6 us
    pallas_call x1, Pallas kernels: 27 us -> 26.6 us  [body(): pl.pallas_call(functools.partial(kernel, n_blk), out_shape=pltpu.VMEM((SH...]
where the time goes in v4:
time: 27.4 us; the launch traced here: 27.3 us
  Pallas kernels  26.6 us (97%)
  local copies, waits for them, and re-layouts  0.66 us (2%)
    pallas_call x1, Pallas kernels, body(): pl.pallas_call(functools.partial(kernel, n_blk), out_shape=pltpu.VMEM((SH...  26.6 us
    unnamed x1, local copies, waits for them, and re-layouts  0.66 us

profile of v4, /device:TPU:1, one launch (start us, length us, event | category | flops | bytes accessed | tf_op | source)
XLA Modules:
  0.0 27.3 jit_solution(18084002279740068947)
XLA Ops:
  0.0 26.6 %shard_map.55 = f32[4,32,256]{2,1,0:T(8,128)S(1)} custom-call(f32[256,768]{1,0:T(8,128)} %amp_hbm.1, f32[256,768]{1,0:T(8,128)} %int_hbm.1, s32[1,768]{1,0:T(1,128)} %cd_hbm.1, s32[1,256]{1,0:T(1,128)} %ab_hbm.1, s32[1,256]{1,0:T(1,128)} %ij_hbm.1), custom_call_target="tpu_custom_call" | custom-call | tf_op jit(solution)/shard_map/pallas_call | solution.py:310
  26.6 0.7 %copy.7 = f32[4,32,256]{2,1,0:T(8,128)} copy(f32[4,32,256]{2,1,0:T(8,128)S(1)} %shard_map.55) | data formatting | bytes 262144

commit v5 on v4

--- a/solution.py
+++ b/solution.py
@@ -13,6 +13,7 @@
 BF16 = jnp.bfloat16
 LANES = 128
 VMEM_LIMIT = 60 * 1024 * 1024
+CUTS = ((0, 104), (104, 96))
 HALF = 200
 
 
@@ -58,7 +59,7 @@
             (int_hbm, integ),
         ))
     ]
-    for load in loads:
+    for load in loads[:4]:
         load.start()
 
     b, r = lax.axis_index("blk"), lax.axis_index("red")
@@ -84,9 +85,8 @@
     pair_columns = [column_of(labels) for labels in pair_labels]
     loads[1].wait()
     cd_labels = cd[...].astype(F32)
-    loads[2].wait()
-    loads[3].wait()
     for h in range(2):
+        loads[2 + h].wait()
         tails = []
         for part in range(2):
             own = pair_columns[h][64 * part : 64 * part + 64]
@@ -95,15 +95,25 @@
             tails.append(tail)
         slabs[0, h, 128:192] = jnp.where(lanes_below(64), *tails)
         slabs[0, h, 192:200] = jnp.broadcast_to(pair_labels[h], (8, LANES))
+    loads[4].start()
+    loads[5].start()
 
     pl.semaphore_wait(barrier, 8)
 
-    def half_copy(h):
-        return pltpu.make_async_remote_copy(
-            src_ref=slabs.at[0, h], dst_ref=slabs.at[2 + h - c, h],
-            send_sem=half_send.at[h], recv_sem=half_recv.at[1 - c],
+    def chunk(m, h, q):
+        return slabs.at[m, h, pl.ds(*CUTS[q])]
+
+    def half_copy(h, q):
+        return pltpu.make_async_remote_copy(
+            src_ref=chunk(0, h, q), dst_ref=chunk(2 + h - c, h, q),
+            send_sem=half_send.at[h, q], recv_sem=half_recv.at[1 - c, q],
             device_id=block(2 + h - c), device_id_type=MESH,
         )
+
+    def send_halves():
+        for h in range(2):
+            for q in range(2):
+                half_copy(h, q).start()
 
     own_copy = pltpu.make_async_remote_copy(
         src_ref=slabs.at[0], dst_ref=slabs.at[1 + 2 * c],
@@ -112,8 +122,7 @@
     )
     @pl.when(k != 2)
     def _():
-        half_copy(0).start()
-        half_copy(1).start()
+        send_halves()
 
     @pl.when(k != 3)
     def _():
@@ -122,32 +131,44 @@
     for y_step in (1, 2, 3):
         pl.semaphore_signal(ready_sem, inc=1, device_id=red(0, y_step), device_id_type=MESH)
 
-    def forward(i):
-        return pltpu.make_async_remote_copy(
-            src_ref=slabs.at[1 + i + c, c], dst_ref=slabs.at[2 + i - c, c],
-            send_sem=fwd_send.at[i], recv_sem=fwd_recv.at[i],
+    def forward(i, q):
+        return pltpu.make_async_remote_copy(
+            src_ref=chunk(1 + i + c, c, q), dst_ref=chunk(2 + i - c, c, q),
+            send_sem=fwd_send.at[i, q], recv_sem=fwd_recv.at[i, q],
             device_id=block(1 - 2 * c), device_id_type=MESH,
         )
 
-    pass_on = pltpu.make_async_remote_copy(
-        src_ref=slabs.at[1 + c, c], dst_ref=slabs.at[3, c],
-        send_sem=pass_send, recv_sem=pass_recv.at[c],
-        device_id=block(2 - c), device_id_type=MESH,
-    )
-
-    def passed(h):
-        return pltpu.make_async_remote_copy(
-            src_ref=slabs.at[0, h], dst_ref=slabs.at[3, h],
-            send_sem=pass_send, recv_sem=pass_recv.at[h],
+    def forwarded(i):
+        for q in range(2):
+            forward(i, q).wait_recv()
+
+    def pass_on(q):
+        return pltpu.make_async_remote_copy(
+            src_ref=chunk(1 + c, c, q), dst_ref=chunk(3, c, q),
+            send_sem=pass_send.at[q], recv_sem=pass_recv.at[c, q],
+            device_id=block(2 - c), device_id_type=MESH,
+        )
+
+    def passed(h, q):
+        return pltpu.make_async_remote_copy(
+            src_ref=chunk(0, h, q), dst_ref=chunk(3, h, q),
+            send_sem=pass_send.at[q], recv_sem=pass_recv.at[h, q],
             device_id=block(-1), device_id_type=MESH,
         )
 
-    def half_arrival(i):
-        return pltpu.make_async_remote_copy(
-            src_ref=slabs.at[0, c], dst_ref=slabs.at[1 + i + c, c],
-            send_sem=half_send.at[0], recv_sem=half_recv.at[i],
+    def half_arrival(i, q):
+        return pltpu.make_async_remote_copy(
+            src_ref=chunk(0, c, q), dst_ref=chunk(1 + i + c, c, q),
+            send_sem=half_send.at[0, q], recv_sem=half_recv.at[i, q],
             device_id=block(2), device_id_type=MESH,
         )
+
+    def from_last_chip(i, hand_on=False):
+        for q in range(2):
+            half_arrival(i, q).wait_recv()
+            if hand_on:
+                pass_on(q).start()
+            forward(i, q).start()
 
     loads[4].wait()
     loads[5].wait()
@@ -221,29 +242,24 @@
         process(m)
         to_peers(m)
 
-    def from_last_chip(i):
-        half_arrival(i).wait_recv()
-        forward(i).start()
-
     process(0)
+
+    @pl.when(k == 2)
+    def _():
+        send_halves()
+
     pl.semaphore_wait(ready_sem, 3)
     to_peers(0)
 
-    @pl.when(k == 2)
-    def _():
-        half_copy(0).start()
-        half_copy(1).start()
-
     @pl.when(k == 0)
     def _():
-        from_last_chip(0)
-        pass_on.start()
+        from_last_chip(0, hand_on=True)
         own_copy.wait_recv()
         shift(3)
         from_last_chip(1)
-        forward(0).wait_recv()
+        forwarded(0)
         shift(1)
-        forward(1).wait_recv()
+        forwarded(1)
         shift(2)
         finish(0)
         finish(3)
@@ -254,13 +270,14 @@
     def _():
         from_last_chip(0)
         from_last_chip(1)
-        forward(0).wait_recv()
+        forwarded(0)
         shift(1)
-        forward(1).wait_recv()
+        forwarded(1)
         shift(2)
         finish(0)
-        passed(0).wait_recv()
-        passed(1).wait_recv()
+        for h in range(2):
+            for q in range(2):
+                passed(h, q).wait_recv()
         shift(3)
         finish(1)
         finish(2)
@@ -270,16 +287,19 @@
     def _():
         own_copy.wait_recv()
         shift(1)
-        from_last_chip(0)
 
         @pl.when(k == 1)
         def _():
-            pass_on.start()
-
-        forward(0).wait_recv()
+            from_last_chip(0, hand_on=True)
+
+        @pl.when(k == 3)
+        def _():
+            from_last_chip(0)
+
+        forwarded(0)
         shift(2)
         from_last_chip(1)
-        forward(1).wait_recv()
+        forwarded(1)
         shift(3)
         finish(0)
         finish(1)
@@ -292,11 +312,13 @@
 
     @pl.when(k < 2)
     def _():
-        pass_on.wait_send()
+        for q in range(2):
+            pass_on(q).wait_send()
 
     for i in range(2):
-        half_copy(i).wait_send()
-        forward(i).wait_send()
+        for q in range(2):
+            half_copy(i, q).wait_send()
+            forward(i, q).wait_send()
     for m in range(SHIFTS):
         all_peers(m).wait_send()
 
@@ -327,12 +349,12 @@
                 pltpu.SemaphoreType.REGULAR,
                 pltpu.SemaphoreType.DMA,
                 pltpu.SemaphoreType.DMA,
+                pltpu.SemaphoreType.DMA((2, 2)),
+                pltpu.SemaphoreType.DMA((2, 2)),
+                pltpu.SemaphoreType.DMA((2, 2)),
+                pltpu.SemaphoreType.DMA((2, 2)),
                 pltpu.SemaphoreType.DMA((2,)),
-                pltpu.SemaphoreType.DMA((2,)),
-                pltpu.SemaphoreType.DMA((2,)),
-                pltpu.SemaphoreType.DMA((2,)),
-                pltpu.SemaphoreType.DMA,
-                pltpu.SemaphoreType.DMA((2,)),
+                pltpu.SemaphoreType.DMA((2, 2)),
                 pltpu.SemaphoreType.DMA((SHIFTS,)),
                 pltpu.SemaphoreType.DMA((SHIFTS,)),
             ],

time: 27.4 us -> 26.7 us (0.974)
  Pallas kernels: 26.6 us -> 25.9 us
    pallas_call x1, Pallas kernels: 26.6 us -> 25.9 us  [body(): pl.pallas_call(functools.partial(kernel, n_blk), out_shape=pltpu.VMEM((SH...]
where the time goes in v5:
time: 26.7 us; the launch traced here: 26.6 us
  Pallas kernels  25.9 us (97%)
  local copies, waits for them, and re-layouts  0.66 us (2%)
    pallas_call x1, Pallas kernels, body(): pl.pallas_call(functools.partial(kernel, n_blk), out_shape=pltpu.VMEM((SH...  25.9 us
    unnamed x1, local copies, waits for them, and re-layouts  0.66 us

profile of v5, /device:TPU:1, one launch (start us, length us, event | category | flops | bytes accessed | tf_op | source)
XLA Modules:
  0.0 26.6 jit_solution(17102052857281590513)
XLA Ops:
  0.0 25.9 %shard_map.55 = f32[4,32,256]{2,1,0:T(8,128)S(1)} custom-call(f32[256,768]{1,0:T(8,128)} %amp_hbm.1, f32[256,768]{1,0:T(8,128)} %int_hbm.1, s32[1,768]{1,0:T(1,128)} %cd_hbm.1, s32[1,256]{1,0:T(1,128)} %ab_hbm.1, s32[1,256]{1,0:T(1,128)} %ij_hbm.1), custom_call_target="tpu_custom_call" | custom-call | tf_op jit(solution)/shard_map/pallas_call | solution.py:332
  26.0 0.7 %copy.7 = f32[4,32,256]{2,1,0:T(8,128)} copy(f32[4,32,256]{2,1,0:T(8,128)S(1)} %shard_map.55) | data formatting | bytes 262144

commit v6 on v5

v6 whole, which is shorter than its diff:
```python
import functools

import jax
import jax.numpy as jnp
from jax import lax
from jax.experimental import pallas as pl
from jax.experimental.pallas import tpu as pltpu
from jax.sharding import PartitionSpec as P

SHIFTS = 4
MESH = pl.DeviceIdType.MESH
F32 = jnp.float32
BF16 = jnp.bfloat16
LANES = 128
NEAR = ((0, 1), (0, 3), (1, 0))
VMEM_LIMIT = 60 * 1024 * 1024
CUTS = ((0, 96), (96, 96))
HALF = 192


def lanes_below(rows):
    return lax.broadcasted_iota(jnp.int32, (rows, LANES), 1) < 64


def column_of(labels):
    return jnp.transpose(jnp.broadcast_to(labels.astype(F32), (LANES, LANES)))


def folded(ref, row, rows, own, cd_labels):
    def kept(t):
        value = ref[pl.ds(row, rows), t * LANES : (t + 1) * LANES]
        return jnp.where(own == cd_labels[:, t * LANES : (t + 1) * LANES], value, 0.0)

    f0, f1, f2 = (kept(t) + kept(t + 3) for t in range(3))
    low = lanes_below(rows)
    head = f0 + pltpu.roll(jnp.where(low, f2, f1), 64, 1)
    tail = jnp.where(low, f1, f2)
    return head, tail + pltpu.roll(tail, 64, 1)


def split(value):
    high = value.astype(BF16)
    return high, (value - high.astype(F32)).astype(BF16)


def kernel(
    n_blk, amp_hbm, int_hbm, cd_hbm, ab_hbm, ij_hbm, out_ref,
    amp, integ, cd, ab, labels, slabs, v_parts, ab_col, send, arrived,
    load_sem, near_sem, far_sem, label_send, label_recv, slab_send, own_recv, half_recv, fwd_recv, pass_recv,
    red_send, red_recv,
):
    loads = [
        pltpu.make_async_copy(src, dst, load_sem.at[i])
        for i, (src, dst) in enumerate((
            (ij_hbm, labels.at[0]),
            (cd_hbm, cd),
            (amp_hbm.at[pl.ds(0, 128)], amp.at[pl.ds(0, 128)]),
            (amp_hbm.at[pl.ds(128, 128)], amp.at[pl.ds(128, 128)]),
            (ab_hbm, ab),
            (int_hbm, integ),
        ))
    ]
    for load in loads[:4]:
        load.start()

    b, r = lax.axis_index("blk"), lax.axis_index("red")
    k = lax.rem(b, 4)
    c = lax.rem(b, 2)
    y, x_hi = lax.rem(r, 4), r // 4

    def block(offset):
        return (lax.rem(b + offset + n_blk, n_blk), r)

    def red(x_step, y_step):
        x_to = 1 - x_hi if x_step else x_hi
        return (b, x_to * 4 + lax.rem(y + y_step, 4))

    barrier = pltpu.get_barrier_semaphore()
    for offset in (-3, -2, -1, 1):
        pl.semaphore_signal(barrier, inc=1, device_id=block(offset), device_id_type=MESH)
    for steps in NEAR:
        pl.semaphore_signal(barrier, inc=1, device_id=red(*steps), device_id_type=MESH)

    def label_copy(m):
        return pltpu.make_async_remote_copy(
            src_ref=labels.at[0], dst_ref=labels.at[m],
            send_sem=label_send, recv_sem=label_recv.at[m - 1],
            device_id=block(m), device_id_type=MESH,
        )

    def chunk(m, h, q):
        return slabs.at[2 * m + h, pl.ds(*CUTS[q])]

    def half_copy(h, q):
        return pltpu.make_async_remote_copy(
            src_ref=chunk(0, h, q), dst_ref=chunk(2 + h - c, h, q),
            send_sem=slab_send, recv_sem=half_recv.at[1 - c, q],
            device_id=block(2 + h - c), device_id_type=MESH,
        )

    def send_half(h):
        for q in range(2):
            half_copy(h, q).start()

    own_copy = pltpu.make_async_remote_copy(
        src_ref=slabs.at[pl.ds(0, 2)], dst_ref=slabs.at[pl.ds(2 + 4 * c, 2)],
        send_sem=slab_send, recv_sem=own_recv,
        device_id=block(1 + 2 * c), device_id_type=MESH,
    )
    loads[0].wait()
    pair_labels = [labels[0, :, 128 * h : 128 * h + 128] for h in range(2)]
    pair_columns = [column_of(row) for row in pair_labels]
    loads[1].wait()
    cd_labels = cd[...].astype(F32)
    loads[2].wait()
    for h in range(2):
        tails = []
        for part in range(2):
            own = pair_columns[h][64 * part : 64 * part + 64]
            head, tail = folded(amp, 128 * h + 64 * part, 64, own, cd_labels)
            slabs[h, 64 * part : 64 * part + 64] = head
            tails.append(tail)
        slabs[h, 128:192] = jnp.where(lanes_below(64), *tails)
        if h == 0:
            loads[3].wait()
            loads[4].start()
            loads[5].start()
            pl.semaphore_wait(barrier, 7)
            for m in (1, 2, 3):
                label_copy(m).start()

        @pl.when(k != 2)
        def _(h=h):
            send_half(h)

    @pl.when(k != 3)
    def _():
        own_copy.start()

    for steps in NEAR:
        pl.semaphore_signal(near_sem, inc=1, device_id=red(*steps), device_id_type=MESH)

    def forward(i, q):
        return pltpu.make_async_remote_copy(
            src_ref=chunk(1 + i + c, c, q), dst_ref=chunk(2 + i - c, c, q),
            send_sem=slab_send, recv_sem=fwd_recv.at[i],
            device_id=block(1 - 2 * c), device_id_type=MESH,
        )

    def forwarded(i):
        pltpu.make_async_remote_copy(
            src_ref=slabs.at[0], dst_ref=slabs.at[0],
            send_sem=slab_send, recv_sem=fwd_recv.at[i],
            device_id=block(1 - 2 * c), device_id_type=MESH,
        ).wait_recv()

    def pass_on(q):
        return pltpu.make_async_remote_copy(
            src_ref=chunk(1 + c, c, q), dst_ref=chunk(3, c, q),
            send_sem=slab_send, recv_sem=pass_recv,
            device_id=block(2 - c), device_id_type=MESH,
        )

    def all_slab_copies(halves):
        return pltpu.make_async_remote_copy(
            src_ref=slabs.at[pl.ds(0, halves)], dst_ref=slabs.at[pl.ds(0, halves)],
            send_sem=slab_send, recv_sem=pass_recv,
            device_id=block(2), device_id_type=MESH,
        )

    def half_arrival(i, q):
        return pltpu.make_async_remote_copy(
            src_ref=chunk(0, c, q), dst_ref=chunk(1 + i + c, c, q),
            send_sem=slab_send, recv_sem=half_recv.at[i, q],
            device_id=block(2), device_id_type=MESH,
        )

    def from_last_chip(i, hand_on=False):
        for q in range(2):
            half_arrival(i, q).wait_recv()
            if hand_on:
                pass_on(q).start()
            forward(i, q).start()

    loads[4].wait()
    loads[5].wait()
    for h in range(2):
        own = column_of(ab[:, 128 * h : 128 * h + 128])
        ab_col[128 * h : 128 * h + 128] = own
        for part in range(2):
            row = 128 * h + 64 * part
            head, tail = folded(integ, row, 64, own[64 * part : 64 * part + 64], cd_labels)
            for t, piece in enumerate((head, jnp.where(lanes_below(64), tail, 0.0))):
                high, low = split(piece)
                for place, value in ((t, high), (t + 2, low), (t + 4, high)):
                    v_parts[row : row + 64, place * LANES : (place + 1) * LANES] = value

    def dot(lhs, rhs):
        return lax.dot_general(lhs, rhs, (((1,), (1,)), ((), ())), preferred_element_type=F32)

    def to_peers(m):
        for x_step in (1, 0):
            for y_step in (2, 1, 3, 0):
                if x_step or y_step:
                    to = red(x_step, y_step)
                    pltpu.make_async_remote_copy(
                        src_ref=send.at[m, to[1]], dst_ref=arrived.at[m, 4 * x_step + y_step - 1],
                        send_sem=red_send, recv_sem=red_recv.at[m],
                        device_id=to, device_id_type=MESH,
                    ).start()

    def all_peers(m):
        return pltpu.make_async_remote_copy(
            src_ref=arrived.at[m], dst_ref=arrived.at[m],
            send_sem=red_send, recv_sem=red_recv.at[m],
            device_id=red(1, 0), device_id_type=MESH,
        )

    def process(m):
        parts = []
        for h in range(2):
            tail = slabs[2 * m + h, 128:192]
            parts.append(jnp.concatenate([slabs[2 * m + h, 0:64], tail], axis=1))
            parts.append(jnp.concatenate([slabs[2 * m + h, 64:128], pltpu.roll(tail, 64, 1)], axis=1))
        high, rest = split(jnp.concatenate(parts, axis=0))
        product = dot(v_parts[...], jnp.concatenate([high, high, rest], axis=1))
        masked = jnp.zeros((256, LANES), F32)
        for h in range(2):
            mask = ab_col[...] == labels[m, :, 128 * h : 128 * h + 128].astype(F32)
            masked = masked + jnp.where(mask, product[:, 128 * h : 128 * h + 128], 0.0)
        twice = masked + pltpu.roll(masked, 64, 1)
        low = lanes_below(16)
        for block_row in range(8):
            row = 32 * block_row
            send[m, block_row] = jnp.where(low, twice[row : row + 16], twice[row + 16 : row + 32])

    def finish(m):
        all_peers(m).wait_recv()
        total = send[m, r]
        for i in range(7):
            total = total + arrived[m, i]
        turned = pltpu.roll(total, 64, 1)
        low = lanes_below(16)
        rows = jnp.concatenate([jnp.where(low, total, turned), jnp.where(low, turned, total)], axis=0)
        own = ab_col[pl.ds(pl.multiple_of(32 * r, 32), 32)]
        for h in range(2):
            mask = own == labels[m, :, 128 * h : 128 * h + 128].astype(F32)
            out_ref[m, :, 128 * h : 128 * h + 128] = jnp.where(mask, rows, 0.0)

    first, second, third = 3 - 2 * c, 1 + c, 2 + c

    def shift(m):
        label_copy(m).wait_recv()
        process(m)
        to_peers(m)

    process(0)

    @pl.when(k == 2)
    def _():
        send_half(0)
        send_half(1)

    pl.semaphore_wait(near_sem, 3)
    pl.semaphore_signal(far_sem, inc=1, device_id=red(0, 3), device_id_type=MESH)
    pl.semaphore_wait(far_sem, 1)
    to_peers(0)

    @pl.when(k == 0)
    def _():
        from_last_chip(0, hand_on=True)
        own_copy.wait_recv()
        shift(3)
        from_last_chip(1)
        forwarded(0)
        shift(1)
        forwarded(1)
        shift(2)
        finish(0)
        finish(3)
        finish(1)
        finish(2)

    @pl.when(k == 2)
    def _():
        from_last_chip(0)
        from_last_chip(1)
        forwarded(0)
        shift(1)
        forwarded(1)
        shift(2)
        finish(0)
        all_slab_copies(2).wait_recv()
        shift(3)
        finish(1)
        finish(2)
        finish(3)

    @pl.when(c == 1)
    def _():
        own_copy.wait_recv()
        shift(1)

        @pl.when(k == 1)
        def _():
            from_last_chip(0, hand_on=True)

        @pl.when(k == 3)
        def _():
            from_last_chip(0)

        forwarded(0)
        shift(2)
        from_last_chip(1)
        forwarded(1)
        shift(3)
        finish(0)
        finish(1)
        finish(2)
        finish(3)

    for halves, blocks in ((7, k < 2), (6, k == 2), (4, k == 3)):
        @pl.when(blocks)
        def _(halves=halves):
            all_slab_copies(halves).wait_send()

    pltpu.make_async_remote_copy(
        src_ref=labels.at[pl.ds(1, 3)], dst_ref=labels.at[pl.ds(1, 3)],
        send_sem=label_send, recv_sem=label_recv.at[0],
        device_id=block(1), device_id_type=MESH,
    ).wait_send()
    pltpu.make_async_remote_copy(
        src_ref=arrived, dst_ref=arrived,
        send_sem=red_send, recv_sem=red_recv.at[0],
        device_id=red(1, 0), device_id_type=MESH,
    ).wait_send()


def solution(mesh):
    n_blk = mesh.shape["blk"]

    def body(amplitudes, integrals, cd_irrep, ab_irrep, ij_irrep):
        vmem = pl.BlockSpec(memory_space=pltpu.VMEM)
        hbm = pl.BlockSpec(memory_space=pltpu.HBM)
        return pl.pallas_call(
            functools.partial(kernel, n_blk),
            out_shape=pltpu.VMEM((SHIFTS, 32, 256), F32),
            in_specs=[hbm] * 5,
            out_specs=vmem,
            scratch_shapes=[
                pltpu.VMEM((256, 768), F32),
                pltpu.VMEM((256, 768), F32),
                pltpu.VMEM((1, 768), jnp.int32),
                pltpu.VMEM((1, 256), jnp.int32),
                pltpu.VMEM((SHIFTS, 1, 256), jnp.int32),
                pltpu.VMEM((2 * SHIFTS, HALF, LANES), F32),
                pltpu.VMEM((256, 768), BF16),
                pltpu.VMEM((256, LANES), F32),
                pltpu.VMEM((SHIFTS, 8, 16, LANES), F32),
                pltpu.VMEM((SHIFTS, 7, 16, LANES), F32),
                pltpu.SemaphoreType.DMA((6,)),
                pltpu.SemaphoreType.REGULAR,
                pltpu.SemaphoreType.REGULAR,
                pltpu.SemaphoreType.DMA,
                pltpu.SemaphoreType.DMA((3,)),
                pltpu.SemaphoreType.DMA,
                pltpu.SemaphoreType.DMA,
                pltpu.SemaphoreType.DMA((2, 2)),
                pltpu.SemaphoreType.DMA((2,)),
                pltpu.SemaphoreType.DMA,
                pltpu.SemaphoreType.DMA,
                pltpu.SemaphoreType.DMA((SHIFTS,)),
            ],
            compiler_params=pltpu.CompilerParams(
                collective_id=0, has_side_effects=True, vmem_limit_bytes=VMEM_LIMIT
            ),
        )(amplitudes, integrals, cd_irrep, ab_irrep, ij_irrep)

    in_specs = (P("blk", "red"), P("blk", "red"), P("red", None), P("blk", None), P("blk", None))
    out_specs = P(None, ("blk", "red"), None)
    return jax.shard_map(body, mesh=mesh, in_specs=in_specs, out_specs=out_specs, check_vma=False)
```

time: 26.7 us -> 26.6 us (level)
  no operation moved by 1% of the time
where the time goes in v6:
time: 26.6 us; the launch traced here: 26.4 us
  Pallas kernels  25.7 us (97%)
  local copies, waits for them, and re-layouts  0.66 us (2%)
    pallas_call x1, Pallas kernels, body(): pl.pallas_call(functools.partial(kernel, n_blk), out_shape=pltpu.VMEM((SH...  25.7 us
    unnamed x1, local copies, waits for them, and re-layouts  0.66 us

profile of v6, /device:TPU:1, one launch (start us, length us, event | category | flops | bytes accessed | tf_op | source)
XLA Modules:
  0.0 26.4 jit_solution(13208339705615886246)
XLA Ops:
  0.0 25.7 %shard_map.55 = f32[4,32,256]{2,1,0:T(8,128)S(1)} custom-call(f32[256,768]{1,0:T(8,128)} %amp_hbm.1, f32[256,768]{1,0:T(8,128)} %int_hbm.1, s32[1,768]{1,0:T(1,128)} %cd_hbm.1, s32[1,256]{1,0:T(1,128)} %ab_hbm.1, s32[1,256]{1,0:T(1,128)} %ij_hbm.1), custom_call_target="tpu_custom_call" | custom-call | tf_op jit(solution)/shard_map/pallas_call | solution.py:345
  25.7 0.7 %copy.7 = f32[4,32,256]{2,1,0:T(8,128)} copy(f32[4,32,256]{2,1,0:T(8,128)S(1)} %shard_map.55) | data formatting | bytes 262144

commit v7 on v6

--- a/solution.py
+++ b/solution.py
@@ -46,7 +46,7 @@
 def kernel(
     n_blk, amp_hbm, int_hbm, cd_hbm, ab_hbm, ij_hbm, out_ref,
     amp, integ, cd, ab, labels, slabs, v_parts, ab_col, send, arrived,
-    load_sem, near_sem, far_sem, label_send, label_recv, slab_send, own_recv, half_recv, fwd_recv, pass_recv,
+    load_sem, reply_sem, near_sem, far_sem, label_send, label_recv, slab_send, own_recv, half_recv, fwd_recv, pass_recv,
     red_send, red_recv,
 ):
     loads = [
@@ -60,7 +60,7 @@
             (int_hbm, integ),
         ))
     ]
-    for load in loads[:4]:
+    for load in loads[:3]:
         load.start()
 
     b, r = lax.axis_index("blk"), lax.axis_index("red")
@@ -78,8 +78,17 @@
     barrier = pltpu.get_barrier_semaphore()
     for offset in (-3, -2, -1, 1):
         pl.semaphore_signal(barrier, inc=1, device_id=block(offset), device_id_type=MESH)
-    for steps in NEAR:
-        pl.semaphore_signal(barrier, inc=1, device_id=red(*steps), device_id_type=MESH)
+    greets = ((y < 2, (0, 1)), (lax.rem(y, 3) == 0, (0, 3)), (x_hi == 0, (1, 0)))
+    answers = ((y >= 2, (0, 1)), (lax.rem(y, 3) != 0, (0, 3)), (x_hi == 1, (1, 0)))
+    greeted_by = lax.rem(y, 2) + 2 * (y // 2) * (1 - lax.rem(y, 2)) + x_hi
+
+    def signal_where(sem, table):
+        for holds, steps in table:
+            @pl.when(holds)
+            def _(steps=steps):
+                pl.semaphore_signal(sem, inc=1, device_id=red(*steps), device_id_type=MESH)
+
+    signal_where(barrier, greets)
 
     def label_copy(m):
         return pltpu.make_async_remote_copy(
@@ -108,12 +117,15 @@
         device_id=block(1 + 2 * c), device_id_type=MESH,
     )
     loads[0].wait()
-    pair_labels = [labels[0, :, 128 * h : 128 * h + 128] for h in range(2)]
-    pair_columns = [column_of(row) for row in pair_labels]
+    loads[3].start()
+    pair_columns = [column_of(labels[0, :, 128 * h : 128 * h + 128]) for h in range(2)]
     loads[1].wait()
     cd_labels = cd[...].astype(F32)
-    loads[2].wait()
     for h in range(2):
+        loads[2 + h].wait()
+        if h == 1:
+            loads[4].start()
+            loads[5].start()
         tails = []
         for part in range(2):
             own = pair_columns[h][64 * part : 64 * part + 64]
@@ -122,10 +134,7 @@
             tails.append(tail)
         slabs[h, 128:192] = jnp.where(lanes_below(64), *tails)
         if h == 0:
-            loads[3].wait()
-            loads[4].start()
-            loads[5].start()
-            pl.semaphore_wait(barrier, 7)
+            pl.semaphore_wait(barrier, 4 + greeted_by)
             for m in (1, 2, 3):
                 label_copy(m).start()
 
@@ -137,8 +146,7 @@
     def _():
         own_copy.start()
 
-    for steps in NEAR:
-        pl.semaphore_signal(near_sem, inc=1, device_id=red(*steps), device_id_type=MESH)
+    signal_where(reply_sem, answers)
 
     def forward(i, q):
         return pltpu.make_async_remote_copy(
@@ -184,6 +192,12 @@
 
     loads[4].wait()
     loads[5].wait()
+
+    @pl.when(k == 2)
+    def _():
+        send_half(0)
+        send_half(1)
+
     for h in range(2):
         own = column_of(ab[:, 128 * h : 128 * h + 128])
         ab_col[128 * h : 128 * h + 128] = own
@@ -256,22 +270,34 @@
 
     process(0)
 
-    @pl.when(k == 2)
-    def _():
-        send_half(0)
-        send_half(1)
+    @pl.when(greeted_by < 3)
+    def _():
+        pl.semaphore_wait(reply_sem, 3 - greeted_by)
+
+    for steps in NEAR:
+        pl.semaphore_signal(near_sem, inc=1, device_id=red(*steps), device_id_type=MESH)
+
+    @pl.when(k == 0)
+    def _():
+        from_last_chip(0, hand_on=True)
 
     pl.semaphore_wait(near_sem, 3)
     pl.semaphore_signal(far_sem, inc=1, device_id=red(0, 3), device_id_type=MESH)
-    pl.semaphore_wait(far_sem, 1)
-    to_peers(0)
+
+    @pl.when(k != 0)
+    def _():
+        pl.semaphore_wait(far_sem, 1)
+        to_peers(0)
 
     @pl.when(k == 0)
     def _():
-        from_last_chip(0, hand_on=True)
         own_copy.wait_recv()
-        shift(3)
+        label_copy(3).wait_recv()
+        process(3)
         from_last_chip(1)
+        pl.semaphore_wait(far_sem, 1)
+        to_peers(0)
+        to_peers(3)
         forwarded(0)
         shift(1)
         forwarded(1)
@@ -361,6 +387,7 @@
                 pltpu.SemaphoreType.DMA((6,)),
                 pltpu.SemaphoreType.REGULAR,
                 pltpu.SemaphoreType.REGULAR,
+                pltpu.SemaphoreType.REGULAR,
                 pltpu.SemaphoreType.DMA,
                 pltpu.SemaphoreType.DMA((3,)),
                 pltpu.SemaphoreType.DMA,

time: 26.6 us -> 26.5 us (level)
  no operation moved by 1% of the time
where the time goes in v7:
time: 26.5 us; the launch traced here: 26.4 us
  Pallas kernels  25.7 us (97%)
  local copies, waits for them, and re-layouts  0.66 us (2%)
    pallas_call x1, Pallas kernels, body(): pl.pallas_call(functools.partial(kernel, n_blk), out_shape=pltpu.VMEM((SH...  25.7 us
    unnamed x1, local copies, waits for them, and re-layouts  0.66 us

profile of v7, /device:TPU:1, one launch (start us, length us, event | category | flops | bytes accessed | tf_op | source)
XLA Modules:
  0.0 26.4 jit_solution(5821090199283531838)
XLA Ops:
  0.0 25.7 %shard_map.55 = f32[4,32,256]{2,1,0:T(8,128)S(1)} custom-call(f32[256,768]{1,0:T(8,128)} %amp_hbm.1, f32[256,768]{1,0:T(8,128)} %int_hbm.1, s32[1,768]{1,0:T(1,128)} %cd_hbm.1, s32[1,256]{1,0:T(1,128)} %ab_hbm.1, s32[1,256]{1,0:T(1,128)} %ij_hbm.1), custom_call_target="tpu_custom_call" | custom-call | tf_op jit(solution)/shard_map/pallas_call | solution.py:371
  25.7 0.7 %copy.7 = f32[4,32,256]{2,1,0:T(8,128)} copy(f32[4,32,256]{2,1,0:T(8,128)S(1)} %shard_map.55) | data formatting | bytes 262144

commit v8 on v6

--- a/solution.py
+++ b/solution.py
@@ -263,12 +263,16 @@
 
     pl.semaphore_wait(near_sem, 3)
     pl.semaphore_signal(far_sem, inc=1, device_id=red(0, 3), device_id_type=MESH)
+
+    @pl.when(k == 0)
+    def _():
+        from_last_chip(0, hand_on=True)
+
     pl.semaphore_wait(far_sem, 1)
     to_peers(0)
 
     @pl.when(k == 0)
     def _():
-        from_last_chip(0, hand_on=True)
         own_copy.wait_recv()
         shift(3)
         from_last_chip(1)

time: 26.6 us -> 26.5 us (level)
  no operation moved by 1% of the time
where the time goes in v8:
time: 26.5 us; the launch traced here: 26.4 us
  Pallas kernels  25.7 us (97%)
  local copies, waits for them, and re-layouts  0.66 us (2%)
    pallas_call x1, Pallas kernels, body(): pl.pallas_call(functools.partial(kernel, n_blk), out_shape=pltpu.VMEM((SH...  25.7 us
    unnamed x1, local copies, waits for them, and re-layouts  0.66 us

profile of v8, /device:TPU:1, one launch (start us, length us, event | category | flops | bytes accessed | tf_op | source)
XLA Modules:
  0.0 26.4 jit_solution(6797823533641317051)
XLA Ops:
  0.0 25.7 %shard_map.55 = f32[4,32,256]{2,1,0:T(8,128)S(1)} custom-call(f32[256,768]{1,0:T(8,128)} %amp_hbm.1, f32[256,768]{1,0:T(8,128)} %int_hbm.1, s32[1,768]{1,0:T(1,128)} %cd_hbm.1, s32[1,256]{1,0:T(1,128)} %ab_hbm.1, s32[1,256]{1,0:T(1,128)} %ij_hbm.1), custom_call_target="tpu_custom_call" | custom-call | tf_op jit(solution)/shard_map/pallas_call | solution.py:349
  25.7 0.7 %copy.7 = f32[4,32,256]{2,1,0:T(8,128)} copy(f32[4,32,256]{2,1,0:T(8,128)S(1)} %shard_map.55) | data formatting | bytes 262144

commit v9 on v6

--- a/solution.py
+++ b/solution.py
@@ -372,7 +372,7 @@
                 pltpu.SemaphoreType.DMA((SHIFTS,)),
             ],
             compiler_params=pltpu.CompilerParams(
-                collective_id=0, has_side_effects=True, vmem_limit_bytes=VMEM_LIMIT
+                collective_id=0, has_side_effects=True, vmem_limit_bytes=VMEM_LIMIT,
             ),
         )(amplitudes, integrals, cd_irrep, ab_irrep, ij_irrep)
 

time: 26.6 us -> 26.6 us (level)
  no operation moved by 1% of the time
where the time goes in v9:
time: 26.6 us; the launch traced here: 26.4 us
  Pallas kernels  25.7 us (97%)
  local copies, waits for them, and re-layouts  0.66 us (2%)
    pallas_call x1, Pallas kernels, body(): pl.pallas_call(functools.partial(kernel, n_blk), out_shape=pltpu.VMEM((SH...  25.7 us
    unnamed x1, local copies, waits for them, and re-layouts  0.66 us

profile of v9, /device:TPU:1, one launch (start us, length us, event | category | flops | bytes accessed | tf_op | source)
XLA Modules:
  0.0 26.4 jit_solution(13208339705615886246)
XLA Ops:
  0.0 25.7 %shard_map.55 = f32[4,32,256]{2,1,0:T(8,128)S(1)} custom-call(f32[256,768]{1,0:T(8,128)} %amp_hbm.1, f32[256,768]{1,0:T(8,128)} %int_hbm.1, s32[1,768]{1,0:T(1,128)} %cd_hbm.1, s32[1,256]{1,0:T(1,128)} %ab_hbm.1, s32[1,256]{1,0:T(1,128)} %ij_hbm.1), custom_call_target="tpu_custom_call" | custom-call | tf_op jit(solution)/shard_map/pallas_call | solution.py:345
  25.7 0.7 %copy.7 = f32[4,32,256]{2,1,0:T(8,128)} copy(f32[4,32,256]{2,1,0:T(8,128)S(1)} %shard_map.55) | data formatting | bytes 262144
